TPU v7x, 32 devices: a whole 2x2x4 slice. The times are simulated.
32 devices in a mesh: dp: 8 (over z, core), tensor: 4 (over y, x).
Axes of the slice: x: 2, y: 2, z: 4, core: 2. Of those that a mesh axis runs over, the one named last changes fastest.
Arguments:
- tokens: bfloat16 [2048, 4096], P('dp', 'tensor'), may hold values from -6 to 6
- cotangent: bfloat16 [2048, 4096], P('dp', 'tensor'), may hold values from -6 to 6
- gate_weight: bfloat16 [4096, 14336], P('dp', 'tensor'), may hold values from -0.09375 to 0.09375
- up_weight: bfloat16 [4096, 14336], P('dp', 'tensor'), may hold values from -0.09375 to 0.09375
- down_weight: bfloat16 [14336, 4096], P('tensor', 'dp'), may hold values from -0.046875 to 0.046875
- counts: int32 [8], replicated, may hold values from 0 to 16, as said below
Outputs:
- outputs: bfloat16 [2048, 4096], P('dp', 'tensor')
- input_grads: bfloat16 [2048, 4096], P('dp', 'tensor')
Inputs may be any that keep to these rules, and one draw needn't show every extreme that they name: counts[r] is the number of live 16-row blocks at the head of rank r's buffer; counts[r] + counts[(r + 4) % 8] = 16 for every rank r, some rank has 16 and some rank has 0.
All inputs are finite; a program needn't handle non-finite values.
Results may differ from a plain program's by a relative error of at most 0.005.
Values may be sent and summed in bfloat16 or wider, within the bound.
A program may use at most 192 MiB of HBM per device.

v0:
```python
import jax
import jax.numpy as jnp
from jax import lax
from jax.sharding import PartitionSpec as P

BLOCK = 16


def passed_along(block, axis, distance):
    devices = range(lax.axis_size(axis))
    route = [((i - distance) % len(devices), i) for i in devices]
    return lax.ppermute(block, axis, route)


def transposed(left, right):
    return lax.dot_general(
        left, right, (((1,), (1,)), ((), ())), preferred_element_type=jnp.float32
    )


def mlp_rows(rows_x, rows_dy, live_rows, gate_full, up_full, down_full):
    whole_x, whole_dy = (
        lax.all_gather(rows_x, "tensor", axis=1, tiled=True),
        lax.all_gather(rows_dy, "tensor", axis=1, tiled=True),
    )
    gate_pre = jnp.dot(whole_x, gate_full, preferred_element_type=jnp.float32)
    up_pre = jnp.dot(whole_x, up_full, preferred_element_type=jnp.float32)
    sigmoid_gate = jax.nn.sigmoid(gate_pre)
    activated = gate_pre * sigmoid_gate
    hidden = (activated * up_pre).astype(jnp.bfloat16)
    partial_y = jnp.dot(hidden, down_full, preferred_element_type=jnp.float32)
    out_rows = lax.psum_scatter(partial_y, "tensor", scatter_dimension=1, tiled=True)
    grad_hidden = transposed(whole_dy, down_full)
    grad_gate = (
        grad_hidden * up_pre * sigmoid_gate * (1.0 + gate_pre * (1.0 - sigmoid_gate))
    ).astype(jnp.bfloat16)
    grad_up = (grad_hidden * activated).astype(jnp.bfloat16)
    partial_dx = transposed(grad_gate, gate_full) + transposed(grad_up, up_full)
    grad_rows = lax.psum_scatter(partial_dx, "tensor", scatter_dimension=1, tiled=True)
    row_mask = live_rows[:, None]
    return ((out_rows * row_mask).astype(jnp.bfloat16), (grad_rows * row_mask).astype(jnp.bfloat16))


def per_device(tokens, cotangent, gate_weight, up_weight, down_weight, counts):
    gate_full, up_full, down_full = (
        lax.all_gather(gate_weight, "dp", axis=0, tiled=True),
        lax.all_gather(up_weight, "dp", axis=0, tiled=True),
        lax.all_gather(down_weight, "dp", axis=1, tiled=True),
    )
    rank_count = lax.axis_size("dp")
    my_rank = lax.axis_index("dp")
    blocks = tokens.shape[0] // BLOCK
    columns = tokens.shape[1]
    own_blocks = counts[my_rank]
    share = blocks // 2
    half_ranks = rank_count // 2
    partner_count = counts[(my_rank + half_ranks) % rank_count]
    upper_x = tokens[share * BLOCK :]
    upper_dy = cotangent[share * BLOCK :]
    got_x, got_dy = passed_along((upper_x, upper_dy), "dp", half_ranks)
    keep_blocks = jnp.minimum(own_blocks, share)
    slot_ids = jnp.arange(share, dtype=jnp.int32)
    foreign = slot_ids - own_blocks
    mine = slot_ids < keep_blocks
    valid = mine | (foreign >= 0) & (foreign < partner_count - share)
    source_index = jnp.where(mine, slot_ids, share + jnp.clip(foreign, 0, share - 1))

    def assemble(lower, received):
        stacked = jnp.concatenate(
            [lower.reshape(share, BLOCK, columns), received.reshape(share, BLOCK, columns)], axis=0
        )
        pieces = jnp.take(stacked, source_index, axis=0)
        pieces = jnp.where(valid[:, None, None], pieces, jnp.zeros_like(pieces))
        return pieces.reshape(share * BLOCK, columns)

    work_x = assemble(tokens[: share * BLOCK], got_x)
    work_dy = assemble(cotangent[: share * BLOCK], got_dy)
    live_rows = jnp.repeat(valid.astype(jnp.float32), BLOCK)
    out_rows, grad_rows = mlp_rows(work_x, work_dy, live_rows, gate_full, up_full, down_full)
    back_pos = own_blocks + slot_ids
    back_ok = back_pos < share
    back_index = jnp.clip(back_pos, 0, share - 1)

    def send_back(source):
        pieces = jnp.take(source.reshape(share, BLOCK, columns), back_index, axis=0)
        pieces = jnp.where(back_ok[:, None, None], pieces, jnp.zeros_like(pieces))
        return pieces.reshape(share * BLOCK, columns)

    back_out, back_grad = passed_along(
        (send_back(out_rows), send_back(grad_rows)), "dp", half_ranks
    )
    upper_live = slot_ids < own_blocks - share

    def home_rows(worked, returned_rows):
        lower = jnp.where(
            mine[:, None, None],
            worked.reshape(share, BLOCK, columns),
            jnp.zeros((share, BLOCK, columns), worked.dtype),
        )
        upper = jnp.where(
            upper_live[:, None, None],
            returned_rows.reshape(share, BLOCK, columns),
            jnp.zeros((share, BLOCK, columns), worked.dtype),
        )
        return jnp.concatenate([lower, upper], axis=0).reshape(blocks * BLOCK, columns)

    outputs = home_rows(out_rows, back_out)
    input_grads = home_rows(grad_rows, back_grad)
    return (outputs, input_grads)


def solution(mesh):
    in_specs = (
        P("dp", "tensor"),
        P("dp", "tensor"),
        P("dp", "tensor"),
        P("dp", "tensor"),
        P("tensor", "dp"),
        P(),
    )
    out_specs = (P("dp", "tensor"), P("dp", "tensor"))
    return jax.shard_map(
        per_device, mesh=mesh, in_specs=in_specs, out_specs=out_specs, check_vma=False
    )
```

profile of v0, /device:TPU:0, one launch (start us, length us, event | category | flops | bytes accessed | tf_op | source)
XLA Modules:
  0.0 1015.0 jit_solution(16153699752031720627)
XLA Ops:
  7.2 0.0 copy-start.2
  7.2 0.0 all-gather.6.cloned.1.call-start
  7.2 1.1 fusion.12
  8.3 4.1 collective-permute-start
  12.4 1.1 fusion.11
  13.5 0.1 collective-permute-start.2
  13.6 0.0 copy-done.2
  13.6 0.6 fusion.13
  15.5 0.6 compare_and_fusion.1
  16.2 14.7 %collective-permute-done = bf16[128,1024]{1,0:T(8,128)(2,1)S(1)} collective-permute-done((bf16[128,1024]{1,0:T(8,128)(2,1)S(1)}, bf16[128,1024]{1,0:T(8,128)(2,1)S(1)}, u32[]{:S(2)}, u32[]{:S(2)}) %collective-permute-start) | collective-permute-done | bytes 262176 | tf_op jit(solution)/shard_map/ppermute | solution.py:12
  30.9 0.6 gather_fusion
  31.4 4.1 collective-permute-done.2
  35.6 0.6 gather_fusion.2
  36.2 0.9 select_select_fusion.1
  37.1 0.0 all-gather.6.cloned.1.call-update
  37.2 0.0 all-gather.10.cloned.1.call-start
  37.2 0.7 all-gather.10.cloned.1.call-update
  37.9 0.0 all-gather.8.cloned.1.call-start
  38.0 0.7 all-gather.8.cloned.1.call-update
  38.6 0.0 all-gather.14.cloned.1.call-start
  38.7 0.5 all-gather.14.cloned.1.call-update
  39.2 0.0 all-gather.12.cloned.1.call-start
  39.3 0.5 all-gather.12.cloned.1.call-update
  39.8 0.0 reduce-scatter.5.cloned.1.call-start
  39.9 25.1 %all-gather.6.cloned.1.call-done = bf16[128,4096]{1,0:T(8,128)(2,1)} async-done(((bf16[128,1024]{1,0:T(8,128)(2,1)}), bf16[128,4096]{1,0:T(8,128)(2,1)}) %all-gather.6.cloned.1.call-update) | async-done | bytes 1048592 | tf_op jit(solution)/shard_map/all_gather | solution.py:23
  65.0 0.0 copy-start.1
  65.0 255.9 %all-gather.10.cloned.1.call-done = bf16[4096,3584]{1,0:T(8,128)(2,1)} async-done(((bf16[512,3584]{1,0:T(8,128)(2,1)}), bf16[4096,3584]{1,0:T(8,128)(2,1)}) %all-gather.10.cloned.1.call-update) | async-done | bytes 29360144 | tf_op jit(solution)/shard_map/all_gather | solution.py:47
  320.9 16.9 %fusion.15 = f32[128,3584]{1,0:T(8,128)} fusion(bf16[128,4096]{1,0:T(8,128)(2,1)} %all-gather.6.cloned.1.call-done, bf16[4096,3584]{1,0:T(8,128)(2,1)} %all-gather.10.cloned.1.call-done), kind=kOutput, calls=%fused_computation.47 | convolution fusion | flops 3758096384 | bytes 32243712 | tf_op jit(solution)/shard_map/dot_general | solution.py:27
  337.8 237.2 %all-gather.8.cloned.1.call-done = bf16[4096,3584]{1,0:T(8,128)(2,1)} async-done(((bf16[512,3584]{1,0:T(8,128)(2,1)}), bf16[4096,3584]{1,0:T(8,128)(2,1)}) %all-gather.8.cloned.1.call-update) | async-done | bytes 29360144 | tf_op jit(solution)/shard_map/all_gather | solution.py:46
  575.0 0.0 copy-done.1
  575.0 11.7 %fusion.14 = f32[128,3584]{1,0:T(8,128)S(1)} fusion(bf16[128,4096]{1,0:T(8,128)(2,1)S(1)} %copy-done.1, bf16[4096,3584]{1,0:T(8,128)(2,1)} %all-gather.8.cloned.1.call-done), kind=kOutput, calls=%fused_computation.46 | convolution fusion | flops 3758096384 | bytes 32243712 | tf_op jit(solution)/shard_map/dot_general | solution.py:26
  586.7 15.3 %all-gather.14.cloned.1.call-done = bf16[128,4096]{1,0:T(8,128)(2,1)} async-done(((bf16[128,1024]{1,0:T(8,128)(2,1)}), bf16[128,4096]{1,0:T(8,128)(2,1)}) %all-gather.14.cloned.1.call-update) | async-done | bytes 1048592 | tf_op jit(solution)/shard_map/all_gather | solution.py:24
  602.0 255.7 %all-gather.12.cloned.1.call-done = bf16[3584,4096]{1,0:T(8,128)(2,1)} async-done(((bf16[3584,512]{1,0:T(8,128)(2,1)}), bf16[3584,4096]{1,0:T(8,128)(2,1)}) %all-gather.12.cloned.1.call-update) | async-done | bytes 29360144 | tf_op jit(solution)/shard_map/all_gather | solution.py:48
  857.7 16.2 %fusion.16 = f32[128,3584]{1,0:T(8,128)} fusion(bf16[128,4096]{1,0:T(8,128)(2,1)} %all-gather.14.cloned.1.call-done, bf16[3584,4096]{1,0:T(8,128)(2,1)} %all-gather.12.cloned.1.call-done), kind=kOutput, calls=%fused_computation.48 | convolution fusion | flops 3758096384 | bytes 32243712 | tf_op jit(solution)/shard_map/dot_general | solution.py:16
  873.9 0.0 copy-start
  873.9 17.0 %fusion.2 = f32[128,4096]{1,0:T(8,128)S(1)} fusion(bf16[4096,3584]{1,0:T(8,128)(2,1)} %all-gather.8.cloned.1.call-done, f32[128,3584]{1,0:T(8,128)S(1)} %fusion.14, f32[128,3584]{1,0:T(8,128)} %fusion.16, f32[128,3584]{1,0:T(8,128)} %fusion.15), kind=kOutput, calls=%fused_computation.11 | convolution fusion | flops 3762683904 | bytes 36962304 | tf_op jit(solution)/shard_map/dot_general | solution.py:16
  890.9 0.0 copy-done
  890.9 15.4 %convolution_add_fusion = f32[128,4096]{1,0:T(8,128)} fusion(f32[128,4096]{1,0:T(8,128)S(1)} %fusion.2, bf16[4096,3584]{1,0:T(8,128)(2,1)} %all-gather.10.cloned.1.call-done, f32[128,3584]{1,0:T(8,128)S(1)} %copy-done, f32[128,3584]{1,0:T(8,128)S(1)} %fusion.14), kind=kOutput, calls=%fused_computation.4 | convolution fusion | flops 3761373184 | bytes 37224448 | tf_op jit(solution)/shard_map/dot_general | solution.py:16
  906.4 0.0 reduce-scatter.5.cloned.1.call-update
  906.4 0.3 reduce-scatter.3.cloned.1.call-start
  906.7 15.8 %fusion.1 = f32[128,4096]{1,0:T(8,128)} fusion(bf16[3584,4096]{1,0:T(8,128)(2,1)} %all-gather.12.cloned.1.call-done, f32[128,3584]{1,0:T(8,128)} %fusion.15, f32[128,3584]{1,0:T(8,128)S(1)} %fusion.14), kind=kOutput, calls=%fused_computation.10 | convolution fusion | flops 3760848896 | bytes 35127296 | tf_op jit(solution)/shard_map/dot_general | solution.py:31
  922.5 0.0 reduce-scatter.3.cloned.1.call-update
  922.5 0.1 broadcast_in_dim.66
  922.6 0.1 mul.39
  923.3 0.6 compare_select_fusion
  923.9 0.6 compare_and_fusion
  924.6 15.3 %reduce-scatter.5.cloned.1.call-done = f32[128,1024]{1,0:T(8,128)} async-done(((f32[128,4096]{1,0:T(8,128)}), f32[128,1024]{1,0:T(8,128)}) %reduce-scatter.5.cloned.1.call-update) | async-done | bytes 524304 | tf_op jit(solution)/shard_map/reduce_scatter | solution.py:39
  939.9 38.2 %reduce-scatter.3.cloned.1.call-done = f32[128,1024]{1,0:T(8,128)} async-done(((f32[128,4096]{1,0:T(8,128)}), f32[128,1024]{1,0:T(8,128)}) %reduce-scatter.3.cloned.1.call-update) | async-done | bytes 524304 | tf_op jit(solution)/shard_map/reduce_scatter | solution.py:32
  978.1 1.3 multiply_convert_fusion.6
  979.4 0.6 gather_fusion.1
  980.0 0.6 gather_fusion.3
  980.5 0.1 select_select_fusion
  980.7 2.5 collective-permute-start.3
  983.2 0.5 collective-permute-start.1
  983.7 0.1 broadcast_select_fusion.2
  983.8 18.0 %collective-permute-done.3 = bf16[128,1024]{1,0:T(8,128)(2,1)S(1)} collective-permute-done((bf16[128,1024]{1,0:T(8,128)(2,1)S(1)}, bf16[128,1024]{1,0:T(8,128)(2,1)S(1)}, u32[]{:S(2)}, u32[]{:S(2)}) %collective-permute-start.3) | collective-permute-done | bytes 262176 | tf_op jit(solution)/shard_map/ppermute | solution.py:12
  1001.8 4.6 collective-permute-done.1
  1006.4 0.1 broadcast_select_fusion
  1006.5 0.8 pad_maximum_fusion.3
  1007.4 0.8 pad_maximum_fusion.1
  (6 shorter events, 0.1 us)
Async XLA Ops:
  7.2 6.4 copy-start.2
  7.2 57.8 %all-gather.6.cloned.1.call-start = ((), (), s32[]{:S(2)}) async-start(), calls=%async_computation.2 | async-start | bytes 1310720 | tf_op jit(solution)/shard_map/all_gather | solution.py:23
  8.3 22.5 %collective-permute-start = (bf16[128,1024]{1,0:T(8,128)(2,1)S(1)}, bf16[128,1024]{1,0:T(8,128)(2,1)S(1)}, u32[]{:S(2)}, u32[]{:S(2)}) collective-permute-start(bf16[128,1024]{1,0:T(8,128)(2,1)S(1)} %get-tuple-element.11), channel_id=1, source_target_pairs={{16,0},{20,4},{24,8},{28,12},{0,16},{4,20},{8,24},{12,28},{17,1},{... | collective-permute-start | bytes 786440 | tf_op jit(solution)/shard_map/ppermute | solution.py:12
  13.5 22.1 %collective-permute-start.2 = (bf16[128,1024]{1,0:T(8,128)(2,1)S(1)}, bf16[128,1024]{1,0:T(8,128)(2,1)S(1)}, u32[]{:S(2)}, u32[]{:S(2)}) collective-permute-start(bf16[128,1024]{1,0:T(8,128)(2,1)S(1)} %get-tuple-element.9), channel_id=1, source_target_pairs={{16,0},{20,4},{24,8},{28,12},{0,16},{4,20},{8,24},{12,28},{17,1},{... | collective-permute-start | bytes 786440 | tf_op jit(solution)/shard_map/ppermute | solution.py:12
  37.2 283.7 %all-gather.10.cloned.1.call-start = ((), (), s32[]{:S(2)}) async-start(), calls=%async_computation.4 | async-start | bytes 33030144 | tf_op jit(solution)/shard_map/all_gather | solution.py:47
  37.9 537.1 %all-gather.8.cloned.1.call-start = ((), (), s32[]{:S(2)}) async-start(), calls=%async_computation.3 | async-start | bytes 33030144 | tf_op jit(solution)/shard_map/all_gather | solution.py:46
  38.6 563.3 %all-gather.14.cloned.1.call-start = ((), (), s32[]{:S(2)}) async-start(), calls=%async_computation.7 | async-start | bytes 1310720 | tf_op jit(solution)/shard_map/all_gather | solution.py:24
  39.2 818.5 %all-gather.12.cloned.1.call-start = ((), (), s32[]{:S(2)}) async-start(), calls=%async_computation.5 | async-start | bytes 33030144 | tf_op jit(solution)/shard_map/all_gather | solution.py:48
  39.8 900.1 %reduce-scatter.5.cloned.1.call-start = ((), (), s32[]{:S(2)}) async-start(), calls=%async_computation.8 | async-start | bytes 2621440 | tf_op jit(solution)/shard_map/reduce_scatter | solution.py:39
  65.0 510.0 %copy-start.1 = (bf16[128,4096]{1,0:T(8,128)(2,1)S(1)}, bf16[128,4096]{1,0:T(8,128)(2,1)}, u32[]{:S(2)}) copy-start(bf16[128,4096]{1,0:T(8,128)(2,1)} %all-gather.6.cloned.1.call-done) | copy-start | bytes 3145732
  873.9 17.0 %copy-start = (f32[128,3584]{1,0:T(8,128)S(1)}, f32[128,3584]{1,0:T(8,128)}, u32[]{:S(2)}) copy-start(f32[128,3584]{1,0:T(8,128)} %fusion.16) | copy-start | bytes 5505028
  906.4 71.7 %reduce-scatter.3.cloned.1.call-start = ((), (), s32[]{:S(2)}) async-start(), calls=%async_computation.6 | async-start | bytes 2621440 | tf_op jit(solution)/shard_map/reduce_scatter | solution.py:32
  980.7 21.1 %collective-permute-start.3 = (bf16[128,1024]{1,0:T(8,128)(2,1)S(1)}, bf16[128,1024]{1,0:T(8,128)(2,1)S(1)}, u32[]{:S(2)}, u32[]{:S(2)}) collective-permute-start(bf16[128,1024]{1,0:T(8,128)(2,1)S(1)} %bitcast.36), channel_id=1, source_target_pairs={{16,0},{20,4},{24,8},{28,12},{0,16},{4,20},{8,24},{12,28},{17,1},{... | collective-permute-start | bytes 786440 | tf_op jit(solution)/shard_map/ppermute | solution.py:12
  983.2 23.2 %collective-permute-start.1 = (bf16[128,1024]{1,0:T(8,128)(2,1)S(1)}, bf16[128,1024]{1,0:T(8,128)(2,1)S(1)}, u32[]{:S(2)}, u32[]{:S(2)}) collective-permute-start(bf16[128,1024]{1,0:T(8,128)(2,1)S(1)} %bitcast.35), channel_id=1, source_target_pairs={{16,0},{20,4},{24,8},{28,12},{0,16},{4,20},{8,24},{12,28},{17,1},{... | collective-permute-start | bytes 786440 | tf_op jit(solution)/shard_map/ppermute | solution.py:12
Sparse Core Ops, SparseCore 0:
  37.3 27.6 all-gather.5
  66.6 254.2 all-gather.9
  322.5 252.3 all-gather.7
  577.3 24.6 all-gather.13
  603.4 254.2 all-gather.11
  906.5 33.3 reduce-scatter.4
  942.9 35.1 reduce-scatter.2
where the time goes:
time: 1020 us
  waiting for transfers between devices  887 us (87%)
  matrix products  93.1 us (9%)
  between operations  16.2 us (2%)
    all_gather x1, waiting for transfers between devices, per_device(): lax.all_gather(up_weight, 'dp', axis=0, tiled=True)  256 us
    all_gather x1, waiting for transfers between devices, per_device(): lax.all_gather(down_weight, 'dp', axis=1, tiled=True)  256 us
    all_gather x1, waiting for transfers between devices, per_device(): lax.all_gather(gate_weight, 'dp', axis=0, tiled=True)  237 us
    dot_general x3, matrix products, transposed(): lax.dot_general(left, right, (((1,), (1,)), ((), ())), preferred_element_...  48.7 us
    ppermute x4, waiting for transfers between devices, passed_along(): return lax.ppermute(block, axis, route)  41.4 us
    reduce_scatter x1, waiting for transfers between devices, mlp_rows(): lax.psum_scatter(partial_y, 'tensor', scatter_dimension=1, tiled=True)  38.2 us
    all_gather x1, waiting for transfers between devices, mlp_rows(): lax.all_gather(rows_x, 'tensor', axis=1, tiled=True)  25.1 us
  transfers between devices with their start and end apart: 11, of which 11 were waited for; matrix products, arithmetic and copies ran while one was open for 5% of the time, Pallas kernels for 0%

commit v1 on v0

--- a/solution.py
+++ b/solution.py
@@ -45,7 +45,7 @@
     gate_full, up_full, down_full = (
         lax.all_gather(gate_weight, "dp", axis=0, tiled=True),
         lax.all_gather(up_weight, "dp", axis=0, tiled=True),
-        lax.all_gather(down_weight, "dp", axis=1, tiled=True),
+        jnp.concatenate(lax.all_gather(down_weight, "dp"), axis=1),
     )
     rank_count = lax.axis_size("dp")
     my_rank = lax.axis_index("dp")

time: 1020 us -> 994 us (0.975)
  waiting for transfers between devices: 887 us -> 838 us
  local copies, waits for them, and re-layouts: 5.19 us -> 39.5 us
    all_gather x1, waiting for transfers between devices: 256 us -> 207 us  [per_device(): lax.all_gather(down_weight, 'dp')]
    reshape x0 -> x1, local copies, waits for them, and re-layouts: none -> 36.1 us  [per_device(): jnp.concatenate(lax.all_gather(down_weight, 'dp'), axis=1)]
    ppermute x4, waiting for transfers between devices: 41.4 us -> 70.5 us  [passed_along(): return lax.ppermute(block, axis, route)]
    all_gather x1, waiting for transfers between devices: 25.1 us -> 0.01 us  [mlp_rows(): lax.all_gather(rows_x, 'tensor', axis=1, tiled=True)]
  transfers between devices with their start and end apart: 11 -> 11, of which waited for: 11 -> 10; matrix products, arithmetic and copies ran while one was open for 5% -> 9% of each run, Pallas kernels for 0% -> 0%
where the time goes in v1:
time: 994 us; the launch traced here: 993 us
  waiting for transfers between devices  838 us (84%)
  matrix products  85.6 us (9%)
  local copies, waits for them, and re-layouts  39.5 us (4%)
  between operations  16.2 us (2%)
    all_gather x1, waiting for transfers between devices, per_device(): lax.all_gather(up_weight, 'dp', axis=0, tiled=True)  250 us
    all_gather x1, waiting for transfers between devices, per_device(): lax.all_gather(gate_weight, 'dp', axis=0, tiled=True)  237 us
    all_gather x1, waiting for transfers between devices, per_device(): lax.all_gather(down_weight, 'dp')  207 us
    ppermute x4, waiting for transfers between devices, passed_along(): return lax.ppermute(block, axis, route)  70.5 us
    dot_general x3, matrix products, transposed(): lax.dot_general(left, right, (((1,), (1,)), ((), ())), preferred_element_...  41.3 us
    reduce_scatter x1, waiting for transfers between devices, mlp_rows(): lax.psum_scatter(partial_y, 'tensor', scatter_dimension=1, tiled=True)  38.2 us
    reshape x1, local copies, waits for them, and re-layouts, per_device(): jnp.concatenate(lax.all_gather(down_weight, 'dp'), axis=1)  36.1 us
  transfers between devices with their start and end apart: 11, of which 10 were waited for; matrix products, arithmetic and copies ran while one was open for 9% of the time, Pallas kernels for 0%

profile of v1, /device:TPU:0, one launch (start us, length us, event | category | flops | bytes accessed | tf_op | source)
XLA Modules:
  0.0 992.9 jit_solution(645505486108477886)
XLA Ops:
  7.2 0.0 all-gather.15.cloned.1.call-start
  7.2 0.0 copy-start.1
  7.2 0.0 copy-start.2
  7.2 0.7 all-gather.15.cloned.1.call-update
  7.9 0.0 copy-start.3
  7.9 0.0 all-gather.7.cloned.1.call-start
  8.0 0.3 copy-done.1
  8.3 4.1 collective-permute-start
  12.4 0.0 copy-done.2
  12.5 0.1 collective-permute-start.2
  12.6 0.0 copy-done.3
  12.6 0.6 fusion.13
  14.5 0.6 compare_and_fusion.1
  15.1 28.3 %collective-permute-done = bf16[128,1024]{1,0:T(8,128)(2,1)S(1)} collective-permute-done((bf16[128,1024]{1,0:T(8,128)(2,1)S(1)}, bf16[128,1024]{1,0:T(8,128)(2,1)S(1)}, u32[]{:S(2)}, u32[]{:S(2)}) %collective-permute-start) | collective-permute-done | bytes 262176 | tf_op jit(solution)/shard_map/ppermute | solution.py:12
  43.5 0.6 gather_fusion
  44.1 19.6 %collective-permute-done.2 = bf16[128,1024]{1,0:T(8,128)(2,1)S(1)} collective-permute-done((bf16[128,1024]{1,0:T(8,128)(2,1)S(1)}, bf16[128,1024]{1,0:T(8,128)(2,1)S(1)}, u32[]{:S(2)}, u32[]{:S(2)}) %collective-permute-start.2) | collective-permute-done | bytes 262176 | tf_op jit(solution)/shard_map/ppermute | solution.py:12
  63.8 0.6 gather_fusion.2
  64.3 0.9 select_select_fusion.1
  65.3 0.0 all-gather.7.cloned.1.call-update
  65.3 0.0 all-gather.11.cloned.1.call-start
  65.3 0.7 all-gather.11.cloned.1.call-update
  66.0 0.0 all-gather.9.cloned.1.call-start
  66.1 0.5 all-gather.9.cloned.1.call-update
  66.6 0.0 all-gather.13.cloned.1.call-start
  66.7 0.5 all-gather.13.cloned.1.call-update
  67.2 0.0 reduce-scatter.5.cloned.1.call-start
  67.2 206.9 %all-gather.15.cloned.1.call-done = bf16[28672,512]{1,0:T(8,128)(2,1)} async-done(((bf16[3584,512]{1,0:T(8,128)(2,1)}), bf16[28672,512]{1,0:T(8,128)(2,1)}) %all-gather.15.cloned.1.call-update) | async-done | bytes 29360144 | tf_op jit(solution)/shard_map/all_gather | solution.py:48
  274.1 36.1 %copy.8 = bf16[3584,8,512]{0,2,1:T(8,128)(2,1)} copy(bf16[3584,8,512]{2,0,1:T(8,128)(2,1)} %bitcast.31) | data formatting | bytes 58720256 | tf_op jit(solution)/shard_map/reshape | solution.py:48
  310.2 0.0 all-gather.7.cloned.1.call-done
  310.2 0.0 copy-start
  310.2 249.9 %all-gather.11.cloned.1.call-done = bf16[4096,3584]{1,0:T(8,128)(2,1)} async-done(((bf16[512,3584]{1,0:T(8,128)(2,1)}), bf16[4096,3584]{1,0:T(8,128)(2,1)}) %all-gather.11.cloned.1.call-update) | async-done | bytes 29360144 | tf_op jit(solution)/shard_map/all_gather | solution.py:47
  560.1 16.9 %fusion.15 = f32[128,3584]{1,0:T(8,128)} fusion(bf16[128,4096]{1,0:T(8,128)(2,1)} %all-gather.7.cloned.1.call-done, bf16[4096,3584]{1,0:T(8,128)(2,1)} %all-gather.11.cloned.1.call-done), kind=kOutput, calls=%fused_computation.47 | convolution fusion | flops 3758096384 | bytes 32243712 | tf_op jit(solution)/shard_map/dot_general | solution.py:27
  577.1 237.0 %all-gather.9.cloned.1.call-done = bf16[4096,3584]{1,0:T(8,128)(2,1)} async-done(((bf16[512,3584]{1,0:T(8,128)(2,1)}), bf16[4096,3584]{1,0:T(8,128)(2,1)}) %all-gather.9.cloned.1.call-update) | async-done | bytes 29360144 | tf_op jit(solution)/shard_map/all_gather | solution.py:46
  814.1 0.0 copy-done
  814.1 11.7 %fusion.14 = f32[128,3584]{1,0:T(8,128)S(1)} fusion(bf16[128,4096]{1,0:T(8,128)(2,1)S(1)} %copy-done, bf16[4096,3584]{1,0:T(8,128)(2,1)} %all-gather.9.cloned.1.call-done), kind=kOutput, calls=%fused_computation.46 | convolution fusion | flops 3758096384 | bytes 32243712 | tf_op jit(solution)/shard_map/dot_general | solution.py:26
  825.8 15.3 %all-gather.13.cloned.1.call-done = bf16[128,4096]{1,0:T(8,128)(2,1)} async-done(((bf16[128,1024]{1,0:T(8,128)(2,1)}), bf16[128,4096]{1,0:T(8,128)(2,1)}) %all-gather.13.cloned.1.call-update) | async-done | bytes 1048592 | tf_op jit(solution)/shard_map/all_gather | solution.py:24
  841.1 11.7 %fusion.16 = f32[128,3584]{1,0:T(8,128)S(1)} fusion(bf16[128,4096]{1,0:T(8,128)(2,1)} %all-gather.13.cloned.1.call-done, bf16[3584,4096]{0,1:T(8,128)(2,1)} %bitcast.29), kind=kOutput, calls=%fused_computation.48 | convolution fusion | flops 3758096384 | bytes 32243712 | tf_op jit(solution)/shard_map/dot_general | solution.py:16
  852.8 13.9 %fusion.2 = f32[128,4096]{1,0:T(8,128)S(1)} fusion(bf16[4096,3584]{1,0:T(8,128)(2,1)} %all-gather.9.cloned.1.call-done, f32[128,3584]{1,0:T(8,128)S(1)} %fusion.14, f32[128,3584]{1,0:T(8,128)S(1)} %fusion.16, f32[128,3584]{1,0:T(8,128)} %fusion.15), kind=kOutput, calls=%fused_computation.11 | convolution fusion | flops 3762683904 | bytes 36962304 | tf_op jit(solution)/shard_map/dot_general | solution.py:16
  866.8 15.6 %convolution_add_fusion = f32[128,4096]{1,0:T(8,128)} fusion(f32[128,4096]{1,0:T(8,128)S(1)} %fusion.2, bf16[4096,3584]{1,0:T(8,128)(2,1)} %all-gather.11.cloned.1.call-done, f32[128,3584]{1,0:T(8,128)S(1)} %fusion.16, f32[128,3584]{1,0:T(8,128)S(1)} %fusion.14), kind=kOutput, calls=%fused_computation.4 | convolution fusion | flops 3761373184 | bytes 37224448 | tf_op jit(solution)/shard_map/dot_general | solution.py:16
  882.4 0.0 reduce-scatter.5.cloned.1.call-update
  882.4 0.0 reduce-scatter.3.cloned.1.call-start
  882.5 15.7 %fusion.1 = f32[128,4096]{1,0:T(8,128)} fusion(bf16[3584,4096]{0,1:T(8,128)(2,1)} %bitcast.30, f32[128,3584]{1,0:T(8,128)} %fusion.15, f32[128,3584]{1,0:T(8,128)S(1)} %fusion.14), kind=kOutput, calls=%fused_computation.10 | convolution fusion | flops 3760848896 | bytes 35127296 | tf_op jit(solution)/shard_map/dot_general | solution.py:31
  898.1 0.0 reduce-scatter.3.cloned.1.call-update
  898.1 0.1 broadcast_in_dim.66
  898.2 0.1 mul.39
  898.9 0.6 compare_select_fusion
  899.6 0.6 compare_and_fusion
  900.2 17.5 %reduce-scatter.5.cloned.1.call-done = f32[128,1024]{1,0:T(8,128)} async-done(((f32[128,4096]{1,0:T(8,128)}), f32[128,1024]{1,0:T(8,128)}) %reduce-scatter.5.cloned.1.call-update) | async-done | bytes 524304 | tf_op jit(solution)/shard_map/reduce_scatter | solution.py:39
  917.8 38.2 %reduce-scatter.3.cloned.1.call-done = f32[128,1024]{1,0:T(8,128)} async-done(((f32[128,4096]{1,0:T(8,128)}), f32[128,1024]{1,0:T(8,128)}) %reduce-scatter.3.cloned.1.call-update) | async-done | bytes 524304 | tf_op jit(solution)/shard_map/reduce_scatter | solution.py:32
  955.9 1.3 multiply_convert_fusion.6
  957.3 0.6 gather_fusion.1
  957.8 0.6 gather_fusion.3
  958.4 0.1 select_select_fusion
  958.6 2.5 collective-permute-start.1
  961.0 0.5 collective-permute-start.3
  961.6 0.1 broadcast_select_fusion.2
  961.7 18.0 %collective-permute-done.1 = bf16[128,1024]{1,0:T(8,128)(2,1)S(1)} collective-permute-done((bf16[128,1024]{1,0:T(8,128)(2,1)S(1)}, bf16[128,1024]{1,0:T(8,128)(2,1)S(1)}, u32[]{:S(2)}, u32[]{:S(2)}) %collective-permute-start.1) | collective-permute-done | bytes 262176 | tf_op jit(solution)/shard_map/ppermute | solution.py:12
  979.7 4.6 collective-permute-done.3
  984.3 0.1 broadcast_select_fusion
  984.4 0.8 pad_maximum_fusion.3
  985.2 0.8 pad_maximum_fusion.1
  (8 shorter events, 0.2 us)
Async XLA Ops:
  7.2 267.0 %all-gather.15.cloned.1.call-start = ((), (), s32[]{:S(2)}) async-start(), calls=%async_computation.8 | async-start | bytes 33030144 | tf_op jit(solution)/shard_map/all_gather | solution.py:48
  7.2 1.0 copy-start.1
  7.2 5.2 copy-start.2
  7.9 4.7 copy-start.3
  7.9 302.3 %all-gather.7.cloned.1.call-start = ((), (), s32[]{:S(2)}) async-start(), calls=%async_computation.2 | async-start | bytes 1310720 | tf_op jit(solution)/shard_map/all_gather | solution.py:23
  8.3 35.2 %collective-permute-start = (bf16[128,1024]{1,0:T(8,128)(2,1)S(1)}, bf16[128,1024]{1,0:T(8,128)(2,1)S(1)}, u32[]{:S(2)}, u32[]{:S(2)}) collective-permute-start(bf16[128,1024]{1,0:T(8,128)(2,1)S(1)} %get-tuple-element.11), channel_id=1, source_target_pairs={{16,0},{20,4},{24,8},{28,12},{0,16},{4,20},{8,24},{12,28},{17,1},{... | collective-permute-start | bytes 786440 | tf_op jit(solution)/shard_map/ppermute | solution.py:12
  12.5 51.3 %collective-permute-start.2 = (bf16[128,1024]{1,0:T(8,128)(2,1)S(1)}, bf16[128,1024]{1,0:T(8,128)(2,1)S(1)}, u32[]{:S(2)}, u32[]{:S(2)}) collective-permute-start(bf16[128,1024]{1,0:T(8,128)(2,1)S(1)} %get-tuple-element.9), channel_id=1, source_target_pairs={{16,0},{20,4},{24,8},{28,12},{0,16},{4,20},{8,24},{12,28},{17,1},{... | collective-permute-start | bytes 786440 | tf_op jit(solution)/shard_map/ppermute | solution.py:12
  65.3 494.8 %all-gather.11.cloned.1.call-start = ((), (), s32[]{:S(2)}) async-start(), calls=%async_computation.4 | async-start | bytes 33030144 | tf_op jit(solution)/shard_map/all_gather | solution.py:47
  66.0 748.0 %all-gather.9.cloned.1.call-start = ((), (), s32[]{:S(2)}) async-start(), calls=%async_computation.3 | async-start | bytes 33030144 | tf_op jit(solution)/shard_map/all_gather | solution.py:46
  66.6 774.5 %all-gather.13.cloned.1.call-start = ((), (), s32[]{:S(2)}) async-start(), calls=%async_computation.6 | async-start | bytes 1310720 | tf_op jit(solution)/shard_map/all_gather | solution.py:24
  67.2 850.6 %reduce-scatter.5.cloned.1.call-start = ((), (), s32[]{:S(2)}) async-start(), calls=%async_computation.7 | async-start | bytes 2621440 | tf_op jit(solution)/shard_map/reduce_scatter | solution.py:39
  310.2 503.8 %copy-start = (bf16[128,4096]{1,0:T(8,128)(2,1)S(1)}, bf16[128,4096]{1,0:T(8,128)(2,1)}, u32[]{:S(2)}) copy-start(bf16[128,4096]{1,0:T(8,128)(2,1)} %all-gather.7.cloned.1.call-done) | copy-start | bytes 3145732
  882.4 73.5 %reduce-scatter.3.cloned.1.call-start = ((), (), s32[]{:S(2)}) async-start(), calls=%async_computation.5 | async-start | bytes 2621440 | tf_op jit(solution)/shard_map/reduce_scatter | solution.py:32
  958.6 21.1 %collective-permute-start.1 = (bf16[128,1024]{1,0:T(8,128)(2,1)S(1)}, bf16[128,1024]{1,0:T(8,128)(2,1)S(1)}, u32[]{:S(2)}, u32[]{:S(2)}) collective-permute-start(bf16[128,1024]{1,0:T(8,128)(2,1)S(1)} %bitcast.43), channel_id=1, source_target_pairs={{16,0},{20,4},{24,8},{28,12},{0,16},{4,20},{8,24},{12,28},{17,1},{... | collective-permute-start | bytes 786440 | tf_op jit(solution)/shard_map/ppermute | solution.py:12
  961.0 23.2 %collective-permute-start.3 = (bf16[128,1024]{1,0:T(8,128)(2,1)S(1)}, bf16[128,1024]{1,0:T(8,128)(2,1)S(1)}, u32[]{:S(2)}, u32[]{:S(2)}) collective-permute-start(bf16[128,1024]{1,0:T(8,128)(2,1)S(1)} %bitcast.42), channel_id=1, source_target_pairs={{16,0},{20,4},{24,8},{28,12},{0,16},{4,20},{8,24},{12,28},{17,1},{... | collective-permute-start | bytes 786440 | tf_op jit(solution)/shard_map/ppermute | solution.py:12
Sparse Core Ops, SparseCore 0:
  9.6 264.4 all-gather.14
  276.5 27.6 all-gather.6
  305.9 254.2 all-gather.10
  561.6 252.3 all-gather.8
  816.3 24.6 all-gather.12
  882.5 35.1 reduce-scatter.4
  920.7 35.1 reduce-scatter.2
